TPU v7x, 32 devices: a whole 2x2x4 slice. The times are simulated.
32 devices in a mesh: shard: 2 (over x), ctx: 4 (over y, core), tp: 4 (over z).
Axes of the slice: x: 2, y: 2, z: 4, core: 2. Of those that a mesh axis runs over, the one named last changes fastest.
Arguments:
- inputs: bfloat16 [2, 2, 4096, 768], P('shard', None, 'ctx'), may hold values from -6 to 6
- lengths: int32 [2, 2], P('shard'), may hold values from 2048 to 4096, as said below
- attn_gain: bfloat16 [768], P('shard'), may hold values from 0.099609375 to 1.8984375
- mlp_gain: bfloat16 [768], P('shard'), may hold values from 0.099609375 to 1.8984375
- qkv_weight: bfloat16 [768, 3, 768], P('shard', None, 'tp'), may hold values from -0.21875 to 0.21875
- attn_weight: bfloat16 [768, 768], P('tp', 'shard'), may hold values from -0.875 to 0.875
- mlp_in_weight: bfloat16 [768, 2, 1152], P('shard', None, 'tp'), may hold values from -0.21875 to 0.21875
- mlp_out_weight: bfloat16 [1152, 768], P('tp', 'shard'), may hold values from -0.1875 to 0.1875
- cotangent: bfloat16 [2, 2, 4096, 768], P('shard', None, 'ctx'), may hold values from -6 to 6
Outputs:
- layer_out: bfloat16 [2, 2, 4096, 768], P('shard', None, 'ctx')
- input_grad: bfloat16 [2, 2, 4096, 768], P('shard', None, 'ctx')
- qkv_grad: float32 [768, 3, 768], P('shard', None, 'tp')
- attn_grad: float32 [768, 768], P('tp', 'shard')
- mlp_in_grad: float32 [768, 2, 1152], P('shard', None, 'tp')
- mlp_out_grad: float32 [1152, 768], P('tp', 'shard')
- attn_gain_grad: float32 [768], P(('shard', 'tp'))
- mlp_gain_grad: float32 [768], P(('shard', 'tp'))
Inputs may be any that keep to these rules, and one draw needn't show every extreme that they name: `lengths`: among the 2 sequences of each index of shard one has length 4096; some sequence has length 2048.
All inputs are finite; a program needn't handle non-finite values.
Results may differ from a plain program's by a relative error of at most 0.017.
Values may be sent and summed in bfloat16 or wider, within the bound.
A program may use at most 192 MiB of HBM per device.

v0:
```python
import math
import jax
import jax.numpy as jnp
from jax import lax
from jax.sharding import PartitionSpec as P

HD = 64
HALF = 64
norm_eps = 1e-05
rope_base = 10000.0
masked_score = -1e30


def padded(cells, sides, width):
    for axis, dim in sides:
        count = lax.axis_size(axis)
        ends = count - 1
        head = lax.slice_in_dim(cells, 0, width, axis=dim)
        tail = lax.slice_in_dim(cells, cells.shape[dim] - width, cells.shape[dim], axis=dim)
        cells = jnp.concatenate(
            [
                lax.ppermute(tail, axis, [(i, (i + 1) % count) for i in range(ends)]),
                cells,
                lax.ppermute(head, axis, [((i + 1) % count, i) for i in range(ends)]),
            ],
            axis=dim,
        )
    return cells


def layer_norm(values, gain_row):
    center = values - jnp.mean(values, axis=-1, keepdims=True)
    variance = jnp.mean(center * center, axis=-1, keepdims=True)
    return center * lax.rsqrt(variance + norm_eps) * gain_row


def rope_tables(positions):
    exponents = jnp.arange(0, HD, 2).astype(jnp.float32) / HD
    inverse = jnp.power(rope_base, -exponents)
    angles = positions[:, None] * inverse[None, :]
    angles = jnp.concatenate([angles, angles], axis=-1)[:, None, :]
    return (jnp.cos(angles), jnp.sin(angles))


def rotate(vector, cosine, sine_table):
    half_size = vector.shape[-1] // 2
    turned = jnp.concatenate([-vector[..., half_size:], vector[..., :half_size]], axis=-1)
    return vector * cosine + turned * sine_table


def geglu(gate_up):
    return jax.nn.gelu(gate_up[..., 0, :], approximate=False) * gate_up[..., 1, :]


def on_device(
    inputs,
    lengths,
    attn_gain,
    mlp_gain,
    qkv_weight,
    attn_weight,
    mlp_in_weight,
    mlp_out_weight,
    cotangent,
):
    gathered = (
        lax.all_gather(qkv_weight, "shard", axis=0, tiled=True),
        lax.all_gather(attn_weight, "shard", axis=1, tiled=True),
        lax.all_gather(mlp_in_weight, "shard", axis=0, tiled=True),
        lax.all_gather(mlp_out_weight, "shard", axis=1, tiled=True),
        lax.all_gather(attn_gain, "shard", axis=0, tiled=True),
        lax.all_gather(mlp_gain, "shard", axis=0, tiled=True),
    )
    qkv_full, attn_full, mlp_in_full, mlp_out_full, attn_gain_low, mlp_gain_low = gathered
    gain_attn = attn_gain_low.astype(jnp.float32)
    gain_mlp = mlp_gain_low.astype(jnp.float32)
    seq_in = inputs[0].astype(jnp.float32)
    batch_count = seq_in.shape[0]
    local_len = seq_in.shape[1]
    tp_width = qkv_full.shape[2]
    local_heads = tp_width // HD
    ext_len = local_len + 2 * HALF
    scaling = 1.0 / math.sqrt(HD)
    query_tile = min(512, local_len)
    tile_count = local_len // query_tile
    key_span = query_tile + 2 * HALF
    ctx_index = lax.axis_index("ctx")
    positions = ctx_index * local_len + jnp.arange(local_len, dtype=jnp.int32)
    seq_lengths = lengths[0]
    valid_rows = (positions[None, :] < seq_lengths[:, None]).astype(jnp.float32)[:, :, None]
    tile_starts = jnp.arange(tile_count, dtype=jnp.int32) * query_tile
    query_pos = (
        ctx_index * local_len
        + tile_starts[:, None]
        + jnp.arange(query_tile, dtype=jnp.int32)[None, :]
    )
    key_pos = (
        ctx_index * local_len
        - HALF
        + tile_starts[:, None]
        + jnp.arange(key_span, dtype=jnp.int32)[None, :]
    )
    distance = query_pos[:, :, None] - key_pos[:, None, :]
    near_keys = (jnp.abs(distance) <= HALF) & (key_pos[:, None, :] >= 0)
    live_keys = (key_pos[None, :, None, :] < seq_lengths[:, None, None, None]) | (distance == 0)[
        None
    ]
    allowed = (near_keys[None] & live_keys)[:, :, None]
    cosine, sine_table = rope_tables(positions.astype(jnp.float32))

    def key_tiles(extended):
        return jnp.stack(
            [
                extended[:, index * query_tile : index * query_tile + key_span]
                for index in range(tile_count)
            ],
            axis=1,
        )

    def untile(tiles):
        total = jnp.zeros((batch_count, ext_len, local_heads, HD), jnp.float32)
        for index in range(tile_count):
            after = ext_len - index * query_tile - key_span
            total = total + jnp.pad(
                tiles[:, index], ((0, 0), (index * query_tile, after), (0, 0), (0, 0))
            )
        return total

    normed_attn, back_norm_attn = jax.vjp(layer_norm, seq_in, gain_attn)
    normed_low = normed_attn.astype(jnp.bfloat16)
    qkv_raw = jnp.einsum("mtd,dcf->mtcf", normed_low, qkv_full, preferred_element_type=jnp.float32)
    heads_raw = qkv_raw.reshape(batch_count, local_len, 3, local_heads, HD)

    def rope_pair(query_raw, key_raw):
        return (rotate(query_raw, cosine, sine_table), rotate(key_raw, cosine, sine_table))

    (query_rot, key_rot), back_rope = jax.vjp(rope_pair, heads_raw[:, :, 0], heads_raw[:, :, 1])
    queries = query_rot.astype(jnp.bfloat16)
    key_value = jnp.stack([key_rot.astype(jnp.bfloat16), heads_raw[:, :, 2].astype(jnp.bfloat16)])
    key_value = key_value.reshape(2, batch_count, local_len, tp_width)
    key_value_ext = padded(key_value, (("ctx", 2),), HALF)
    key_value_ext = key_value_ext.reshape(2, batch_count, ext_len, local_heads, HD)
    keys_tiled = key_tiles(key_value_ext[0])
    values_tiled = key_tiles(key_value_ext[1])
    queries_tiled = queries.reshape(batch_count, tile_count, query_tile, local_heads, HD)

    def masked_scores():
        raw_scores = (
            jnp.einsum(
                "mnqhd,mnkhd->mnhqk", queries_tiled, keys_tiled, preferred_element_type=jnp.float32
            )
            * scaling
        )
        return jnp.where(allowed, raw_scores, masked_score)

    scores = masked_scores()
    top_score = jnp.max(scores, axis=-1, keepdims=True)
    exponent_terms = jnp.exp(scores - top_score)
    denominator = jnp.sum(exponent_terms, axis=-1, keepdims=True)
    soft_low = (exponent_terms / denominator).astype(jnp.bfloat16)
    log_total = top_score + jnp.log(denominator)
    context = jnp.einsum(
        "mnhqk,mnkhd->mnqhd", soft_low, values_tiled, preferred_element_type=jnp.float32
    )
    context_low = context.astype(jnp.bfloat16).reshape(batch_count, local_len, tp_width)
    attn_part = jnp.einsum(
        "mtf,fd->mtd", context_low, attn_full, preferred_element_type=jnp.float32
    )
    attn_out = lax.psum(attn_part, "tp")
    middle = seq_in + attn_out
    normed_mlp, back_norm_mlp = jax.vjp(layer_norm, middle, gain_mlp)
    normed_mlp_low = normed_mlp.astype(jnp.bfloat16)
    gate_up = jnp.einsum(
        "mtd,dcf->mtcf", normed_mlp_low, mlp_in_full, preferred_element_type=jnp.float32
    )
    hidden, back_glu = jax.vjp(geglu, gate_up)
    hidden_low = hidden.astype(jnp.bfloat16)
    mlp_part = jnp.einsum(
        "mtf,fd->mtd", hidden_low, mlp_out_full, preferred_element_type=jnp.float32
    )
    mlp_out = lax.psum(mlp_part.astype(jnp.bfloat16), "tp").astype(jnp.float32)
    layer_out = ((middle + mlp_out) * valid_rows).astype(jnp.bfloat16)[None]
    grad_out = cotangent[0].astype(jnp.float32) * valid_rows
    grad_out_low = grad_out.astype(jnp.bfloat16)
    mlp_out_grad = jnp.einsum(
        "mtf,mtd->fd", hidden_low, grad_out_low, preferred_element_type=jnp.float32
    )
    grad_hidden = jnp.einsum(
        "mtd,fd->mtf", grad_out_low, mlp_out_full, preferred_element_type=jnp.float32
    )
    (grad_gate_up,) = back_glu(grad_hidden)
    grad_gate_low = grad_gate_up.astype(jnp.bfloat16)
    mlp_in_grad = jnp.einsum(
        "mtd,mtcf->dcf", normed_mlp_low, grad_gate_low, preferred_element_type=jnp.float32
    )
    grad_mlp_part = jnp.einsum(
        "mtcf,dcf->mtd", grad_gate_low, mlp_in_full, preferred_element_type=jnp.float32
    )
    grad_normed_mlp = lax.psum(grad_mlp_part, "tp")
    grad_mid_norm, mlp_gain_grad = back_norm_mlp(grad_normed_mlp)
    grad_middle = grad_out + grad_mid_norm
    grad_middle_low = grad_middle.astype(jnp.bfloat16)
    attn_grad = jnp.einsum(
        "mtf,mtd->fd", context_low, grad_middle_low, preferred_element_type=jnp.float32
    )
    grad_context = jnp.einsum(
        "mtd,fd->mtf", grad_middle_low, attn_full, preferred_element_type=jnp.float32
    )
    grad_context = grad_context.astype(jnp.bfloat16).reshape(
        batch_count, tile_count, query_tile, local_heads, HD
    )
    soft_again = jnp.exp(masked_scores() - log_total)
    soft_again_low = soft_again.astype(jnp.bfloat16)
    grad_values = jnp.einsum(
        "mnhqk,mnqhd->mnkhd", soft_again_low, grad_context, preferred_element_type=jnp.float32
    )
    grad_soft = jnp.einsum(
        "mnqhd,mnkhd->mnhqk", grad_context, values_tiled, preferred_element_type=jnp.float32
    )
    row_terms = jnp.sum(soft_again * grad_soft, axis=-1, keepdims=True)
    grad_scores = (soft_again * (grad_soft - row_terms)).astype(jnp.bfloat16)
    grad_queries = (
        jnp.einsum(
            "mnhqk,mnkhd->mnqhd", grad_scores, keys_tiled, preferred_element_type=jnp.float32
        )
        * scaling
    )
    grad_queries = grad_queries.reshape(batch_count, local_len, local_heads, HD)
    grad_keys = (
        jnp.einsum(
            "mnhqk,mnqhd->mnkhd", grad_scores, queries_tiled, preferred_element_type=jnp.float32
        )
        * scaling
    )
    grad_ext = jnp.stack([untile(grad_keys), untile(grad_values)]).reshape(
        2, batch_count, ext_len, tp_width
    )
    rim_pairs = jnp.concatenate([grad_ext[:, :, :HALF], grad_ext[:, :, ext_len - HALF :]], axis=2)
    arrived = padded(rim_pairs, (("ctx", 2),), HALF)
    from_lower = arrived[:, :, :HALF]
    from_upper = arrived[:, :, arrived.shape[2] - HALF :]
    grad_own = grad_ext[:, :, HALF : HALF + local_len]
    grad_own = grad_own + jnp.pad(from_lower, ((0, 0), (0, 0), (0, local_len - HALF), (0, 0)))
    grad_own = grad_own + jnp.pad(from_upper, ((0, 0), (0, 0), (local_len - HALF, 0), (0, 0)))
    grad_key_rot = grad_own[0].reshape(batch_count, local_len, local_heads, HD)
    grad_value_own = grad_own[1].reshape(batch_count, local_len, local_heads, HD)
    grad_query_raw, grad_key_raw = back_rope((grad_queries, grad_key_rot))
    grad_qkv = jnp.stack([grad_query_raw, grad_key_raw, grad_value_own], axis=2)
    grad_qkv_low = grad_qkv.reshape(batch_count, local_len, 3, tp_width).astype(jnp.bfloat16)
    qkv_grad = jnp.einsum(
        "mtd,mtcf->dcf", normed_low, grad_qkv_low, preferred_element_type=jnp.float32
    )
    grad_attn_part = jnp.einsum(
        "mtcf,dcf->mtd", grad_qkv_low, qkv_full, preferred_element_type=jnp.float32
    )
    grad_normed = lax.psum(grad_attn_part, "tp")
    grad_in_norm, attn_gain_grad = back_norm_attn(grad_normed)
    input_grad = (grad_middle + grad_in_norm).astype(jnp.bfloat16)[None]
    partials = (qkv_grad, attn_grad, mlp_in_grad, mlp_out_grad, attn_gain_grad, mlp_gain_grad)
    summed = lax.psum(
        (partials[0], partials[1], partials[2], partials[3], partials[4], partials[5]), "ctx"
    )
    reduced = (
        lax.psum_scatter(summed[0], "shard", scatter_dimension=0, tiled=True),
        lax.psum_scatter(summed[1], "shard", scatter_dimension=1, tiled=True),
        lax.psum_scatter(summed[2], "shard", scatter_dimension=0, tiled=True),
        lax.psum_scatter(summed[3], "shard", scatter_dimension=1, tiled=True),
        lax.psum_scatter(summed[4], "shard", scatter_dimension=0, tiled=True),
        lax.psum_scatter(summed[5], "shard", scatter_dimension=0, tiled=True),
    )
    gain_share = reduced[4].shape[0] // lax.axis_size("tp")
    gain_start = lax.axis_index("tp") * gain_share
    attn_gain_out = lax.dynamic_slice_in_dim(reduced[4], gain_start, gain_share)
    mlp_gain_out = lax.dynamic_slice_in_dim(reduced[5], gain_start, gain_share)
    return (
        layer_out,
        input_grad,
        reduced[0],
        reduced[1],
        reduced[2],
        reduced[3],
        attn_gain_out,
        mlp_gain_out,
    )


def solution(mesh):
    in_specs = (
        P("shard", None, "ctx", None),
        P("shard", None),
        P("shard"),
        P("shard"),
        P("shard", None, "tp"),
        P("tp", "shard"),
        P("shard", None, "tp"),
        P("tp", "shard"),
        P("shard", None, "ctx", None),
    )
    out_specs = (
        P("shard", None, "ctx", None),
        P("shard", None, "ctx", None),
        P("shard", None, "tp"),
        P("tp", "shard"),
        P("shard", None, "tp"),
        P("tp", "shard"),
        P(("shard", "tp")),
        P(("shard", "tp")),
    )
    return jax.shard_map(
        on_device, mesh=mesh, in_specs=in_specs, out_specs=out_specs, check_vma=False
    )
```

profile of v0, /device:TPU:0, one launch (start us, length us, event | category | flops | bytes accessed | tf_op | source)
XLA Modules:
  0.0 1094.5 jit_solution(6729855262283549967)
XLA Ops:
  8.1 5.3 all-gather
  17.6 11.8 %all_gather.19 = bf16[768,3,192]{0,2,1:T(8,128)(2,1)S(1)} all-gather(bf16[384,3,192]{0,2,1:T(8,128)(2,1)S(1)} %copy-done.45), channel_id=1, replica_groups=mesh['shard'=2,'ctx'=4,'tp'=4] {'shard'}, dimensions={0}, use_global_device_ids=true | all-gather | bytes 1327104 | tf_op jit(solution)/shard_map/all_gather | solution.py:67
  60.4 7.3 all_gather.20
  85.1 5.0 fusion.106
  104.9 6.9 all_gather.23
  111.8 12.6 %all_gather.22 = bf16[768,2,288]{0,2,1:T(8,128)(2,1)} all-gather(bf16[384,2,288]{0,2,1:T(8,128)(2,1)} %param.15), channel_id=1, replica_groups=mesh['shard'=2,'ctx'=4,'tp'=4] {'shard'}, dimensions={0}, use_global_device_ids=true | all-gather | bytes 1327104 | tf_op jit(solution)/shard_map/all_gather | solution.py:69
  129.1 194.1 %all-reduce.23.cloned.1.call-done = f32[2,1024,768]{2,1,0:T(8,128)} async-done(((f32[2,1024,768]{2,1,0:T(8,128)}), f32[2,1024,768]{2,1,0:T(8,128)}) %all-reduce.23.cloned.1.call-update) | async-done | bytes 6291472 | tf_op jit(solution)/shard_map/psum | solution.py:169
  332.0 5.1 multiply_bitcast_fusion
  345.3 6.4 convolution_convert_fusion
  353.6 9.3 fusion.103
  363.9 7.7 fusion.96
  371.7 194.6 %all-reduce.27.cloned.1.call-done = f32[2,1024,768]{2,1,0:T(8,128)} async-done(((f32[2,1024,768]{2,1,0:T(8,128)}), f32[2,1024,768]{2,1,0:T(8,128)}) %all-reduce.27.cloned.1.call-update) | async-done | bytes 6291472 | tf_op jit(solution)/shard_map/psum | solution.py:199
  566.3 6.2 multiply_reduce_fusion.1
  572.5 116.8 %all-reduce.25.cloned.1.call-done = bf16[2,1024,768]{2,1,0:T(8,128)(2,1)} async-done(((bf16[2,1024,768]{2,1,0:T(8,128)(2,1)}), bf16[2,1024,768]{2,1,0:T(8,128)(2,1)}) %all-reduce.25.cloned.1.call-update) | async-done | bytes 3145744 | tf_op jit(solution)/shard_map/psum | solution.py:181
  689.3 8.3 fusion.174
  707.5 14.0 %multiply_reduce_fusion = (f32[2,2,3,512]{3,2,1,0:T(4,128)S(1)}, f32[2,2,3,512,640]{4,3,2,1,0:T(8,128)}) fusion(f32[2,2,3,512,640]{4,3,2,1,0:T(8,128)} %copy-done, f32[2,2,3,512]{3,2,1,0:T(4,128)S(1)} %log_add_fusion, bf16[2,1,640,3,64]{2,4,3,1,0:T(8,128)(2,1)} %copy-done.33, bf16[2,1,640,3,64]{2,4,3,1,0:T(8,128)(2,1)} %copy-done.32, ...), kind=kOutput, calls=%fused_computation.1 | convolution fusion | flops 515598336 | bytes 33275904 | tf_op jit(solution)/shard_map/mnqhd,mnkhd->mnhqk/dot_general | solution.py:217
  722.7 7.4 multiply_convert_fusion
  761.0 7.3 convolution_bitcast_fusion
  770.3 25.6 %reduce-scatter.5.cloned.1.call-done = f32[384,3,192]{0,2,1:T(8,128)} async-done(((f32[768,3,192]{0,2,1:T(8,128)}), f32[384,3,192]{0,2,1:T(8,128)}) %reduce-scatter.5.cloned.1.call-update) | async-done | bytes 884752 | tf_op jit(solution)/shard_map/reduce_scatter | solution.py:264
  795.9 225.4 %all-reduce.29.cloned.1.call-done = f32[2,1024,768]{2,1,0:T(8,128)} async-done(((f32[2,1024,768]{2,1,0:T(8,128)}), f32[2,1024,768]{2,1,0:T(8,128)}) %all-reduce.29.cloned.1.call-update) | async-done | bytes 6291472 | tf_op jit(solution)/shard_map/psum | solution.py:256
  1029.1 5.0 all-reduce.16
  1034.2 6.7 all-reduce.14
  1042.1 9.2 fusion.30
  1051.3 30.6 %all-reduce.31.cloned.1.call-done = (f32[384,3,192]{0,2,1:T(8,128)}, f32[192,384]{1,0:T(8,128)}, f32[384,2,288]{0,2,1:T(8,128)}, f32[288,384]{1,0:T(8,128)}) async-done(((f32[384,3,192]{0,2,1:T(8,128)}, f32[192,384]{1,0:T(8,128)}, f32[384,2,288]{0,2,1:T(8,128)}, f32[288,384]{1,0:T(8,128)}), (f32[384,3,192]{0,2,1:T(8,128)}, f32[192,384]{1,0:T(8,128)}, f32[384,2,288]{0,2,1:T(8,128)}, ...) | async-done | bytes 2506768 | tf_op jit(solution)/shard_map/psum | solution.py:260
  (254 shorter events, 150.0 us)
Async XLA Ops:
  7.2 316.0 %all-reduce.23.cloned.1.call-start = ((), (), s32[]{:S(2)}) async-start(), calls=%async_computation.4 | async-start | bytes 12582912 | tf_op jit(solution)/shard_map/psum | solution.py:169
  13.4 15.9 %copy-start.54 = (f32[768]{0:T(1024)}, f32[768]{0:T(1024)S(1)}, u32[]{:S(2)}) copy-start(f32[768]{0:T(1024)S(1)} %reshape.411) | copy-start | bytes 9220
  15.9 16.1 %copy-start.46 = (f32[2,1024]{1,0:T(2,128)}, f32[2,1024]{1,0:T(2,128)S(1)}, u32[]{:S(2)}) copy-start(f32[2,1024]{1,0:T(2,128)S(1)} %broadcast_multiply_fusion.5) | copy-start | bytes 24580
  17.6 14.4 %copy-start.52 = (f32[2,1024]{1,0:T(2,128)}, f32[2,1024]{1,0:T(2,128)S(1)}, u32[]{:S(2)}) copy-start(f32[2,1024]{1,0:T(2,128)S(1)} %fusion.130) | copy-start | bytes 24580
  42.4 25.3 %collective-permute-start.1 = (bf16[2,2,64,192]{2,3,1,0:T(8,128)(2,1)}, bf16[2,2,64,192]{2,3,1,0:T(8,128)(2,1)}, u32[]{:S(2)}, u32[]{:S(2)}) collective-permute-start(bf16[2,2,64,192]{2,3,1,0:T(8,128)(2,1)} %get-tuple-element.43), channel_id=1, source_target_pairs={{4,0},{8,4},{12,8},{5,1},{9,5},{13,9},{6,2},{10,6},{14,10},{7,3},{... | collective-permute-start | bytes 294920 | tf_op jit(solution)/shard_map/ppermute | solution.py:24
  43.7 24.0 %collective-permute-start = (bf16[2,2,64,192]{2,3,1,0:T(8,128)(2,1)}, bf16[2,2,64,192]{2,3,1,0:T(8,128)(2,1)}, u32[]{:S(2)}, u32[]{:S(2)}) collective-permute-start(bf16[2,2,64,192]{2,3,1,0:T(8,128)(2,1)} %get-tuple-element.44), channel_id=1, source_target_pairs={{0,4},{4,8},{8,12},{1,5},{5,9},{9,13},{2,6},{6,10},{10,14},{3,7},{... | collective-permute-start | bytes 294920 | tf_op jit(solution)/shard_map/ppermute | solution.py:22
  73.9 8.9 copy-start.32
  74.0 8.9 copy-start.33
  99.9 466.4 %all-reduce.27.cloned.1.call-start = ((), (), s32[]{:S(2)}) async-start(), calls=%async_computation.6 | async-start | bytes 12582912 | tf_op jit(solution)/shard_map/psum | solution.py:199
  111.8 12.7 %copy-start.34 = (bf16[288,768]{1,0:T(8,128)(2,1)}, bf16[288,768]{1,0:T(8,128)(2,1)S(1)}, u32[]{:S(2)}) copy-start(bf16[288,768]{1,0:T(8,128)(2,1)S(1)} %all_gather.23) | copy-start | bytes 1327108
  344.4 345.0 %all-reduce.25.cloned.1.call-start = ((), (), s32[]{:S(2)}) async-start(), calls=%async_computation.5 | async-start | bytes 6291456 | tf_op jit(solution)/shard_map/psum | solution.py:181
  351.7 418.5 %reduce-scatter.11.cloned.1.call-start = ((), (), s32[]{:S(2)}) async-start(), calls=%async_computation.11 | async-start | bytes 1327104 | tf_op jit(solution)/shard_map/reduce_scatter | solution.py:267
  362.9 407.3 %reduce-scatter.9.cloned.1.call-start = ((), (), s32[]{:S(2)}) async-start(), calls=%async_computation.10 | async-start | bytes 2654208 | tf_op jit(solution)/shard_map/reduce_scatter | solution.py:266
  371.7 398.6 %reduce-scatter.7.cloned.1.call-start = ((), (), s32[]{:S(2)}) async-start(), calls=%async_computation.9 | async-start | bytes 884736 | tf_op jit(solution)/shard_map/reduce_scatter | solution.py:265
  704.1 17.4 %slice-start = ((s8[15728640]{0:T(1024)(128)(4,1)}), s8[3145728]{0:T(1024)(128)(4,1)S(1)}, s32[]{:S(2)}) async-start(s8[15728640]{0:T(1024)(128)(4,1)} %bitcast.348), calls=%async_computation.13 | async-start | bytes 6291456
  707.5 14.0 %slice-start.1 = ((s8[15728640]{0:T(1024)(128)(4,1)}), s8[4194304]{0:T(1024)(128)(4,1)S(1)}, s32[]{:S(2)}) async-start(s8[15728640]{0:T(1024)(128)(4,1)} %bitcast.348), calls=%async_computation.14 | async-start | bytes 8388608
  707.5 14.0 %slice-start.2 = ((s8[15728640]{0:T(1024)(128)(4,1)}), s8[4194304]{0:T(1024)(128)(4,1)S(1)}, s32[]{:S(2)}) async-start(s8[15728640]{0:T(1024)(128)(4,1)} %bitcast.348), calls=%async_computation.15 | async-start | bytes 8388608
  707.5 15.2 %slice-start.3 = ((s8[15728640]{0:T(1024)(128)(4,1)}), s8[4194304]{0:T(1024)(128)(4,1)S(1)}, s32[]{:S(2)}) async-start(s8[15728640]{0:T(1024)(128)(4,1)} %bitcast.348), calls=%async_computation.16 | async-start | bytes 8388608
  743.0 5.6 collective-permute-start.2
  745.6 4.5 collective-permute-start.3
  748.5 47.3 %reduce-scatter.5.cloned.1.call-start = ((), (), s32[]{:S(2)}) async-start(), calls=%async_computation.8 | async-start | bytes 2654208 | tf_op jit(solution)/shard_map/reduce_scatter | solution.py:264
  760.9 260.3 %all-reduce.29.cloned.1.call-start = ((), (), s32[]{:S(2)}) async-start(), calls=%async_computation.7 | async-start | bytes 12582912 | tf_op jit(solution)/shard_map/psum | solution.py:256
  768.3 313.6 %all-reduce.31.cloned.1.call-start = ((), (), s32[]{:S(2)}) async-start(), calls=%async_computation.12 | async-start | bytes 5013504 | tf_op jit(solution)/shard_map/psum | solution.py:260
  795.9 229.3 %copy-start.51 = (f32[2,1024]{1,0:T(2,128)S(1)}, f32[2,1024]{1,0:T(2,128)}, u32[]{:S(2)}) copy-start(f32[2,1024]{1,0:T(2,128)} %copy-done.50) | copy-start | bytes 24580
  (53 other events, 147.5 us)
Sparse Core Ops, SparseCore 0:
  100.0 223.1 all-reduce.22
  344.5 221.7 all-reduce.26
  569.3 120.0 all-reduce.24
  692.0 17.5 reduce-scatter.10
  711.7 28.2 reduce-scatter.8
  748.6 16.0 reduce-scatter.6
  767.6 28.2 reduce-scatter.4
  798.3 222.8 all-reduce.28
  1024.0 57.8 all-reduce.30
where the time goes:
time: 1100 us; the launch traced here: 1090 us
  waiting for transfers between devices  789 us (72%)
  matrix products  88.2 us (8%)
  other arithmetic  76 us (7%)
  blocking collectives  60 us (5%)
  local copies, waits for them, and re-layouts  56.3 us (5%)
  between operations  15.9 us (1%)
    psum x1, waiting for transfers between devices, on_device(): grad_normed = lax.psum(grad_attn_part, 'tp')  225 us
    psum x1, waiting for transfers between devices, on_device(): grad_normed_mlp = lax.psum(grad_mlp_part, 'tp')  195 us
    psum x1, waiting for transfers between devices, on_device(): attn_out = lax.psum(attn_part, 'tp')  194 us
    psum x1, waiting for transfers between devices, on_device(): mlp_out = lax.psum(mlp_part.astype(jnp.bfloat16), 'tp').astype(jnp.float32)  117 us
    psum x1, waiting for transfers between devices, on_device(): lax.psum((partials[0], partials[1], partials[2], partials[3], partials[4]...  30.6 us
    unnamed x137, local copies, waits for them, and re-layouts  29.4 us
    reduce_scatter x1, waiting for transfers between devices, on_device(): lax.psum_scatter(summed[0], 'shard', scatter_dimension=0, tiled=True)  25.6 us
  transfers between devices with their start and end apart: 13, of which 7 were waited for; matrix products, arithmetic and copies ran while one was open for 12% of the time, Pallas kernels for 0%

commit v1 on v0

--- a/solution.py
+++ b/solution.py
@@ -196,7 +196,7 @@
     grad_mlp_part = jnp.einsum(
         "mtcf,dcf->mtd", grad_gate_low, mlp_in_full, preferred_element_type=jnp.float32
     )
-    grad_normed_mlp = lax.psum(grad_mlp_part, "tp")
+    grad_normed_mlp = jnp.sum(lax.all_gather(grad_mlp_part, "tp"), axis=0)
     grad_mid_norm, mlp_gain_grad = back_norm_mlp(grad_normed_mlp)
     grad_middle = grad_out + grad_mid_norm
     grad_middle_low = grad_middle.astype(jnp.bfloat16)

time: 1100 us -> 1310 us (1.19)
  waiting for transfers between devices: 789 us -> 975 us
    all_gather x0 -> x1, waiting for transfers between devices: none -> 395 us  [on_device(): grad_normed_mlp = jnp.sum(lax.all_gather(grad_mlp_part, 'tp'), axis=0)]
    psum x1 -> x0, waiting for transfers between devices: 195 us -> none  [on_device(): grad_normed_mlp = lax.psum(grad_mlp_part, 'tp')]
    psum x1, waiting for transfers between devices: 117 us -> 103 us  [on_device(): mlp_out = lax.psum(mlp_part.astype(jnp.bfloat16), 'tp').astype(jnp.float32)]
  transfers between devices with their start and end apart: 13 -> 13, of which waited for: 7 -> 7; matrix products, arithmetic and copies ran while one was open for 12% -> 11% of each run, Pallas kernels for 0% -> 0%
where the time goes in v1:
time: 1310 us; the launch traced here: 1300 us
  waiting for transfers between devices  975 us (74%)
  matrix products  89.4 us (7%)
  other arithmetic  88.9 us (7%)
  blocking collectives  60 us (5%)
  local copies, waits for them, and re-layouts  57.1 us (4%)
  between operations  15.9 us (1%)
    all_gather x1, waiting for transfers between devices, on_device(): grad_normed_mlp = jnp.sum(lax.all_gather(grad_mlp_part, 'tp'), axis=0)  395 us
    psum x1, waiting for transfers between devices, on_device(): grad_normed = lax.psum(grad_attn_part, 'tp')  225 us
    psum x1, waiting for transfers between devices, on_device(): attn_out = lax.psum(attn_part, 'tp')  194 us
    psum x1, waiting for transfers between devices, on_device(): mlp_out = lax.psum(mlp_part.astype(jnp.bfloat16), 'tp').astype(jnp.float32)  103 us
    psum x1, waiting for transfers between devices, on_device(): lax.psum((partials[0], partials[1], partials[2], partials[3], partials[4]...  30.6 us
    unnamed x137, local copies, waits for them, and re-layouts  30.2 us
  transfers between devices with their start and end apart: 13, of which 7 were waited for; matrix products, arithmetic and copies ran while one was open for 11% of the time, Pallas kernels for 0%

profile of v1, /device:TPU:0, one launch (start us, length us, event | category | flops | bytes accessed | tf_op | source)
XLA Modules:
  0.0 1296.2 jit_solution(11746763267222441335)
XLA Ops:
  8.1 5.3 all-gather.1
  17.6 11.8 all_gather.25
  60.4 7.3 all_gather.26
  85.0 5.0 fusion.106
  104.9 6.9 all_gather.29
  111.8 12.7 all_gather.28
  129.1 194.1 %all-reduce.22.cloned.1.call-done = f32[2,1024,768]{2,1,0:T(8,128)} async-done(((f32[2,1024,768]{2,1,0:T(8,128)}), f32[2,1024,768]{2,1,0:T(8,128)}) %all-reduce.22.cloned.1.call-update) | async-done | bytes 6291472 | tf_op jit(solution)/shard_map/psum | solution.py:169
  332.1 5.1 multiply_bitcast_fusion
  345.6 6.5 convolution_convert_fusion
  354.8 9.5 fusion.103
  365.4 8.4 fusion.96
  373.8 395.0 %all-gather.5.cloned.1.call-done = f32[8,1024,768]{2,1,0:T(8,128)} async-done(((f32[2,1024,768]{2,1,0:T(8,128)}), f32[8,1024,768]{2,1,0:T(8,128)}) %all-gather.5.cloned.1.call-update) | async-done | bytes 25165840 | tf_op jit(solution)/shard_map/all_gather | solution.py:199
  768.8 12.9 reduce_sum.121
  781.7 6.3 multiply_reduce_fusion.1
  788.0 103.1 %all-reduce.24.cloned.1.call-done = bf16[2,1024,768]{2,1,0:T(8,128)(2,1)} async-done(((bf16[2,1024,768]{2,1,0:T(8,128)(2,1)}), bf16[2,1024,768]{2,1,0:T(8,128)(2,1)}) %all-reduce.24.cloned.1.call-update) | async-done | bytes 3145744 | tf_op jit(solution)/shard_map/psum | solution.py:181
  891.1 8.3 fusion.174
  909.2 14.0 %multiply_reduce_fusion = (f32[2,2,3,512]{3,2,1,0:T(4,128)S(1)}, f32[2,2,3,512,640]{4,3,2,1,0:T(8,128)}) fusion(f32[2,2,3,512,640]{4,3,2,1,0:T(8,128)} %copy-done, f32[2,2,3,512]{3,2,1,0:T(4,128)S(1)} %log_add_fusion, bf16[2,1,640,3,64]{2,4,3,1,0:T(8,128)(2,1)} %copy-done.33, bf16[2,1,640,3,64]{2,4,3,1,0:T(8,128)(2,1)} %copy-done.32, ...), kind=kOutput, calls=%fused_computation.1 | convolution fusion | flops 515598336 | bytes 33275904 | tf_op jit(solution)/shard_map/mnqhd,mnkhd->mnhqk/dot_general | solution.py:217
  924.4 7.4 multiply_convert_fusion
  962.6 7.3 convolution_bitcast_fusion
  971.9 25.7 %reduce-scatter.5.cloned.1.call-done = f32[384,3,192]{0,2,1:T(8,128)} async-done(((f32[768,3,192]{0,2,1:T(8,128)}), f32[384,3,192]{0,2,1:T(8,128)}) %reduce-scatter.5.cloned.1.call-update) | async-done | bytes 884752 | tf_op jit(solution)/shard_map/reduce_scatter | solution.py:264
  997.6 225.3 %all-reduce.26.cloned.1.call-done = f32[2,1024,768]{2,1,0:T(8,128)} async-done(((f32[2,1024,768]{2,1,0:T(8,128)}), f32[2,1024,768]{2,1,0:T(8,128)}) %all-reduce.26.cloned.1.call-update) | async-done | bytes 6291472 | tf_op jit(solution)/shard_map/psum | solution.py:256
  1235.9 6.7 all-reduce.14
  1243.8 9.2 fusion.30
  1253.0 30.6 %all-reduce.28.cloned.1.call-done = (f32[384,3,192]{0,2,1:T(8,128)}, f32[192,384]{1,0:T(8,128)}, f32[384,2,288]{0,2,1:T(8,128)}, f32[288,384]{1,0:T(8,128)}) async-done(((f32[384,3,192]{0,2,1:T(8,128)}, f32[192,384]{1,0:T(8,128)}, f32[384,2,288]{0,2,1:T(8,128)}, f32[288,384]{1,0:T(8,128)}), (f32[384,3,192]{0,2,1:T(8,128)}, f32[192,384]{1,0:T(8,128)}, f32[384,2,288]{0,2,1:T(8,128)}, ...) | async-done | bytes 2506768 | tf_op jit(solution)/shard_map/psum | solution.py:260
  (255 shorter events, 155.9 us)
Async XLA Ops:
  7.2 316.1 %all-reduce.22.cloned.1.call-start = ((), (), s32[]{:S(2)}) async-start(), calls=%async_computation.4 | async-start | bytes 12582912 | tf_op jit(solution)/shard_map/psum | solution.py:169
  13.4 15.9 %copy-start.54 = (f32[768]{0:T(1024)}, f32[768]{0:T(1024)S(1)}, u32[]{:S(2)}) copy-start(f32[768]{0:T(1024)S(1)} %reshape.412) | copy-start | bytes 9220
  15.9 16.1 %copy-start.46 = (f32[2,1024]{1,0:T(2,128)}, f32[2,1024]{1,0:T(2,128)S(1)}, u32[]{:S(2)}) copy-start(f32[2,1024]{1,0:T(2,128)S(1)} %broadcast_multiply_fusion.5) | copy-start | bytes 24580
  17.6 14.4 %copy-start.52 = (f32[2,1024]{1,0:T(2,128)}, f32[2,1024]{1,0:T(2,128)S(1)}, u32[]{:S(2)}) copy-start(f32[2,1024]{1,0:T(2,128)S(1)} %fusion.130) | copy-start | bytes 24580
  42.4 25.3 %collective-permute-start.1 = (bf16[2,2,64,192]{2,3,1,0:T(8,128)(2,1)}, bf16[2,2,64,192]{2,3,1,0:T(8,128)(2,1)}, u32[]{:S(2)}, u32[]{:S(2)}) collective-permute-start(bf16[2,2,64,192]{2,3,1,0:T(8,128)(2,1)} %get-tuple-element.43), channel_id=1, source_target_pairs={{4,0},{8,4},{12,8},{5,1},{9,5},{13,9},{6,2},{10,6},{14,10},{7,3},{... | collective-permute-start | bytes 294920 | tf_op jit(solution)/shard_map/ppermute | solution.py:24
  43.7 24.0 %collective-permute-start = (bf16[2,2,64,192]{2,3,1,0:T(8,128)(2,1)}, bf16[2,2,64,192]{2,3,1,0:T(8,128)(2,1)}, u32[]{:S(2)}, u32[]{:S(2)}) collective-permute-start(bf16[2,2,64,192]{2,3,1,0:T(8,128)(2,1)} %get-tuple-element.44), channel_id=1, source_target_pairs={{0,4},{4,8},{8,12},{1,5},{5,9},{9,13},{2,6},{6,10},{10,14},{3,7},{... | collective-permute-start | bytes 294920 | tf_op jit(solution)/shard_map/ppermute | solution.py:22
  73.9 8.9 copy-start.32
  73.9 8.9 copy-start.33
  99.9 668.9 %all-gather.5.cloned.1.call-start = ((), (), s32[]{:S(2)}) async-start(), calls=%async_computation.7 | async-start | bytes 31457280 | tf_op jit(solution)/shard_map/all_gather | solution.py:199
  111.8 12.7 copy-start.34
  344.6 546.5 %all-reduce.24.cloned.1.call-start = ((), (), s32[]{:S(2)}) async-start(), calls=%async_computation.5 | async-start | bytes 6291456 | tf_op jit(solution)/shard_map/psum | solution.py:181
  352.1 619.8 %reduce-scatter.11.cloned.1.call-start = ((), (), s32[]{:S(2)}) async-start(), calls=%async_computation.11 | async-start | bytes 1327104 | tf_op jit(solution)/shard_map/reduce_scatter | solution.py:267
  364.4 607.5 %reduce-scatter.9.cloned.1.call-start = ((), (), s32[]{:S(2)}) async-start(), calls=%async_computation.10 | async-start | bytes 2654208 | tf_op jit(solution)/shard_map/reduce_scatter | solution.py:266
  373.8 598.1 %reduce-scatter.7.cloned.1.call-start = ((), (), s32[]{:S(2)}) async-start(), calls=%async_computation.9 | async-start | bytes 884736 | tf_op jit(solution)/shard_map/reduce_scatter | solution.py:265
  905.8 17.4 %slice-start = ((s8[15728640]{0:T(1024)(128)(4,1)}), s8[3145728]{0:T(1024)(128)(4,1)S(1)}, s32[]{:S(2)}) async-start(s8[15728640]{0:T(1024)(128)(4,1)} %bitcast.349), calls=%async_computation.13 | async-start | bytes 6291456
  909.2 14.0 %slice-start.1 = ((s8[15728640]{0:T(1024)(128)(4,1)}), s8[4194304]{0:T(1024)(128)(4,1)S(1)}, s32[]{:S(2)}) async-start(s8[15728640]{0:T(1024)(128)(4,1)} %bitcast.349), calls=%async_computation.14 | async-start | bytes 8388608
  909.2 14.0 %slice-start.2 = ((s8[15728640]{0:T(1024)(128)(4,1)}), s8[4194304]{0:T(1024)(128)(4,1)S(1)}, s32[]{:S(2)}) async-start(s8[15728640]{0:T(1024)(128)(4,1)} %bitcast.349), calls=%async_computation.15 | async-start | bytes 8388608
  909.2 15.2 %slice-start.3 = ((s8[15728640]{0:T(1024)(128)(4,1)}), s8[4194304]{0:T(1024)(128)(4,1)S(1)}, s32[]{:S(2)}) async-start(s8[15728640]{0:T(1024)(128)(4,1)} %bitcast.349), calls=%async_computation.16 | async-start | bytes 8388608
  944.6 5.6 collective-permute-start.2
  947.2 4.5 collective-permute-start.3
  950.2 47.3 %reduce-scatter.5.cloned.1.call-start = ((), (), s32[]{:S(2)}) async-start(), calls=%async_computation.8 | async-start | bytes 2654208 | tf_op jit(solution)/shard_map/reduce_scatter | solution.py:264
  962.5 260.4 %all-reduce.26.cloned.1.call-start = ((), (), s32[]{:S(2)}) async-start(), calls=%async_computation.6 | async-start | bytes 12582912 | tf_op jit(solution)/shard_map/psum | solution.py:256
  969.9 313.7 %all-reduce.28.cloned.1.call-start = ((), (), s32[]{:S(2)}) async-start(), calls=%async_computation.12 | async-start | bytes 5013504 | tf_op jit(solution)/shard_map/psum | solution.py:260
  997.6 229.3 %copy-start.51 = (f32[2,1024]{1,0:T(2,128)S(1)}, f32[2,1024]{1,0:T(2,128)}, u32[]{:S(2)}) copy-start(f32[2,1024]{1,0:T(2,128)} %copy-done.50) | copy-start | bytes 24580
  (53 other events, 148.1 us)
Sparse Core Ops, SparseCore 0:
  100.0 223.1 all-reduce.21
  344.7 424.0 all-gather.4
  771.8 119.2 all-reduce.23
  893.8 17.5 reduce-scatter.10
  913.5 28.2 reduce-scatter.8
  950.3 16.0 reduce-scatter.6
  969.3 28.2 reduce-scatter.4
  1000.0 222.8 all-reduce.25
  1225.7 57.8 all-reduce.27
